TPU v7x, 32 devices: a whole 2x2x4 slice. The times are simulated.
32 devices in a mesh: grp: 2 (over core), cores: 16 (over z, y, x).
Axes of the slice: x: 2, y: 2, z: 4, core: 2. Of those that a mesh axis runs over, the one named last changes fastest.
Arguments:
- rhs_core: float32 [4, 8192], P(None, 'cores'), may hold values from -6 to 6
- rhs_noncore: float32 [4, 8192], P(None, ('grp', 'cores')), may hold values from -6 to 6
- records_core: float32 [4, 8192], P(None, 'cores'), may hold values from 0.2 to 2
- records_noncore: float32 [4, 8192], P(None, ('grp', 'cores')), may hold values from 0.2 to 2
- core_inverse: bfloat16 [8192, 8192], P('cores'), as said below
- genomic_block: bfloat16 [8192, 8192], P(('grp', 'cores')), may hold values from -0.125 to 0.125
- m_inverse: float32 [8192], P(('grp', 'cores')), may hold values from 0.5 to 4
- trait_inverse: float32 [4, 4], replicated, as said below
Outputs:
- sol_core: float32 [4, 8192], P(None, 'cores')
- sol_noncore: float32 [4, 8192], P(None, ('grp', 'cores'))
- res_core: float32 [4, 8192], P(None, 'cores')
- res_noncore: float32 [4, 8192], P(None, ('grp', 'cores'))
Inputs may be any that keep to these rules, and one draw needn't show every extreme that they name: core_inverse is symmetric and positive definite. trait_inverse is symmetric and positive definite.
All inputs are finite; a program needn't handle non-finite values.
Results may differ from a plain program's by a relative error of at most 0.028.
Values may be sent and summed in bfloat16 or wider, within the bound.
No kernel may reach another device: no remote copies, remote signals or barrier semaphores. Data moves between devices by JAX's collectives and lax.ppermute only.
A program may use at most 64 MiB of HBM per device.

v0:
```python
import jax
import jax.numpy as jnp
from jax import lax
from jax.sharding import PartitionSpec as P

ITERS = 2


def genomic_map(core_vec, non_vec, core_inverse, genomic_block, m_inverse):
    core_in = core_vec.astype(jnp.bfloat16)
    partial_map = jnp.dot(core_in, core_inverse, preferred_element_type=jnp.float32)
    mapped = lax.psum(partial_map, "cores")
    mapped_in = mapped.astype(jnp.bfloat16)
    pulled = lax.dot_general(
        mapped_in, genomic_block, (((1,), (1,)), ((), ())), preferred_element_type=jnp.float32
    )
    scaled = m_inverse[None, :] * (non_vec - pulled)
    pushed_part = jnp.dot(
        scaled.astype(jnp.bfloat16), genomic_block, preferred_element_type=jnp.float32
    )
    grouped = lax.psum(pushed_part.astype(jnp.bfloat16), "grp")
    pushed = lax.psum_scatter(grouped, "cores", scatter_dimension=1, tiled=True).astype(jnp.float32)
    remainder = (core_vec - pushed).astype(jnp.bfloat16)
    back_part = jnp.dot(remainder, core_inverse, preferred_element_type=jnp.float32)
    core_out = lax.psum_scatter(
        back_part.astype(jnp.bfloat16), "cores", scatter_dimension=1, tiled=True
    ).astype(jnp.float32)
    return (core_out, scaled)


def body(
    rhs_core,
    rhs_noncore,
    records_core,
    records_noncore,
    core_inverse,
    genomic_block,
    m_inverse,
    trait_inverse,
):
    highest = lax.Precision.HIGHEST
    first_copy = (lax.axis_index("grp") == 0).astype(jnp.float32)
    trait_diag = jnp.diagonal(trait_inverse)[:, None]
    prec_core = 1.0 / (records_core + trait_diag)
    prec_non = 1.0 / (records_noncore + trait_diag * m_inverse[None, :])
    sol_core = jnp.zeros_like(rhs_core)
    sol_non = jnp.zeros_like(rhs_noncore)
    res_core, res_non = (rhs_core, rhs_noncore)
    z_core, z_non = (prec_core * res_core, prec_non * res_non)
    dir_core, dir_non = (z_core, z_non)

    def residual_inner(core_a, core_b, non_a, non_b):
        local_sum = jnp.sum(non_a * non_b) + first_copy * jnp.sum(core_a * core_b)
        return lax.psum(local_sum, ("grp", "cores"))

    rz_now = residual_inner(res_core, z_core, res_non, z_non)
    for iteration in range(ITERS):
        core_out, non_out = genomic_map(dir_core, dir_non, core_inverse, genomic_block, m_inverse)
        image_core = records_core * dir_core + jnp.dot(trait_inverse, core_out, precision=highest)
        image_non = records_noncore * dir_non + jnp.dot(trait_inverse, non_out, precision=highest)
        local_curve = jnp.sum(dir_non * image_non) + first_copy * jnp.sum(dir_core * image_core)
        step_size = rz_now / lax.psum(local_curve, ("grp", "cores"))
        sol_core = sol_core + step_size * dir_core
        sol_non = sol_non + step_size * dir_non
        res_core = res_core - step_size * image_core
        res_non = res_non - step_size * image_non
        if iteration + 1 < ITERS:
            z_core, z_non = (prec_core * res_core, prec_non * res_non)
            rz_next = residual_inner(res_core, z_core, res_non, z_non)
            factor = rz_next / rz_now
            dir_core = z_core + factor * dir_core
            dir_non = z_non + factor * dir_non
            rz_now = rz_next
    return (sol_core, sol_non, res_core, res_non)


def solution(mesh):
    in_specs = (
        P(None, "cores"),
        P(None, ("grp", "cores")),
        P(None, "cores"),
        P(None, ("grp", "cores")),
        P("cores", None),
        P(("grp", "cores"), None),
        P(("grp", "cores")),
        P(),
    )
    out_specs = (
        P(None, "cores"),
        P(None, ("grp", "cores")),
        P(None, "cores"),
        P(None, ("grp", "cores")),
    )
    return jax.shard_map(body, mesh=mesh, in_specs=in_specs, out_specs=out_specs, check_vma=False)
```

profile of v0, /device:TPU:12, one launch (start us, length us, event | category | flops | bytes accessed | tf_op | source)
XLA Modules:
  0.0 657.4 jit_solution(4603464972572962994)
XLA Ops:
  9.3 4.6 fusion.12
  13.9 67.9 %all-reduce.3 = bf16[4,8192]{1,0:T(4,128)(2,1)S(1)} all-reduce(f32[4,8192]{1,0:T(4,128)S(1)} %fusion.12), channel_id=1, replica_groups=mesh['grp'=2,'cores'=16] {'cores'}, use_global_device_ids=true, to_apply=%region_3.4 | all-reduce | flops 32768 | bytes 196608 | tf_op jit(solution)/shard_map/psum | solution.py:12
  81.9 3.5 fusion.5
  86.1 1.9 copy.16
  88.1 78.8 %reduce-scatter.17.cloned.1.call-done = bf16[512,4]{1,0:T(8,128)(2,1)} async-done(((bf16[8192,4]{1,0:T(8,128)(2,1)}), bf16[512,4]{1,0:T(8,128)(2,1)}) %reduce-scatter.17.cloned.1.call-update) | async-done | bytes 4112
  166.9 1.0 copy.17
  167.9 2.5 psum.64
  170.4 4.6 convolution_convert_fusion.2
  174.9 1.9 copy.12
  177.7 77.5 %reduce-scatter.13.cloned.1.call-done = bf16[512,4]{1,0:T(8,128)(2,1)} async-done(((bf16[8192,4]{1,0:T(8,128)(2,1)}), bf16[512,4]{1,0:T(8,128)(2,1)}) %reduce-scatter.13.cloned.1.call-update) | async-done | bytes 4112
  255.2 1.7 multiply_reduce_fusion.2
  259.5 48.3 %all-reduce = (f32[]{:T(128)}, f32[]{:T(128)}) all-reduce(f32[]{:T(128)S(6)} %add.78, f32[]{:T(128)S(6)} %add.81), channel_id=1, replica_groups=mesh['grp'=2,'cores'=16] {'grp','cores'}, use_global_device_ids=true, to_apply=%region_2.3 | all-reduce | flops 2 | bytes 16 | tf_op jit(solution)/shard_map/psum | solution.py:54
  311.8 38.3 %psum.60 = f32[]{:T(128)} all-reduce(f32[]{:T(128)S(6)} %add.82), channel_id=1, replica_groups=mesh['grp'=2,'cores'=16] {'grp','cores'}, use_global_device_ids=true, to_apply=%region_12.13 | all-reduce | flops 1 | bytes 8 | tf_op jit(solution)/shard_map/psum | solution.py:54
  351.5 4.6 fusion.10
  356.1 67.8 %all-reduce.4 = bf16[4,8192]{1,0:T(4,128)(2,1)S(1)} all-reduce(f32[4,8192]{1,0:T(4,128)S(1)} %fusion.10), channel_id=1, replica_groups=mesh['grp'=2,'cores'=16] {'cores'}, use_global_device_ids=true, to_apply=%region_13.14 | all-reduce | flops 32768 | bytes 196608 | tf_op jit(solution)/shard_map/psum | solution.py:12
  423.9 3.5 fusion.3
  428.1 1.9 copy.18
  430.1 78.8 %reduce-scatter.19.cloned.1.call-done = bf16[512,4]{1,0:T(8,128)(2,1)} async-done(((bf16[8192,4]{1,0:T(8,128)(2,1)}), bf16[512,4]{1,0:T(8,128)(2,1)}) %reduce-scatter.19.cloned.1.call-update) | async-done | bytes 4112
  509.8 2.5 psum.65
  512.3 4.6 convolution_convert_fusion
  516.9 1.9 copy.14
  519.5 77.7 %reduce-scatter.15.cloned.1.call-done = bf16[512,4]{1,0:T(8,128)(2,1)} async-done(((bf16[8192,4]{1,0:T(8,128)(2,1)}), bf16[512,4]{1,0:T(8,128)(2,1)}) %reduce-scatter.15.cloned.1.call-update) | async-done | bytes 4112
  597.2 1.7 multiply_reduce_fusion
  600.2 48.1 %psum.63 = f32[]{:T(128)} all-reduce(f32[]{:T(128)S(6)} %add.87), channel_id=1, replica_groups=mesh['grp'=2,'cores'=16] {'grp','cores'}, use_global_device_ids=true, to_apply=%region_19.20 | all-reduce | flops 1 | bytes 8 | tf_op jit(solution)/shard_map/psum | solution.py:62
  (39 shorter events, 8.9 us)
Async XLA Ops:
  7.2 0.7 copy-start
  7.2 159.7 %reduce-scatter.17.cloned.1.call-start = ((), (), s32[]{:S(2)}) async-start(), calls=%async_computation.6 | async-start | bytes 2228224
  9.3 72.5 %copy-start.5 = (f32[4,256]{1,0:T(4,128)S(1)}, f32[4,256]{1,0:T(4,128)}, u32[]{:S(2)}) copy-start(f32[4,256]{1,0:T(4,128)} %param.11) | copy-start | bytes 12292
  9.3 72.5 %copy-start.6 = (f32[4,256]{1,0:T(4,128)S(1)}, f32[4,256]{1,0:T(4,128)}, u32[]{:S(2)}) copy-start(f32[4,256]{1,0:T(4,128)} %param.9) | copy-start | bytes 12292
  9.3 72.5 %copy-start.7 = (f32[256]{0:T(256)S(1)}, f32[256]{0:T(256)}, u32[]{:S(2)}) copy-start(f32[256]{0:T(256)} %param.14) | copy-start | bytes 3076
  81.8 3.6 copy-start.1
  88.0 167.1 %reduce-scatter.13.cloned.1.call-start = ((), (), s32[]{:S(2)}) async-start(), calls=%async_computation.4 | async-start | bytes 2228224
  174.9 80.2 %copy-start.3 = (f32[4,512]{1,0:T(4,128)S(1)}, f32[4,512]{1,0:T(4,128)}, u32[]{:S(2)}) copy-start(f32[4,512]{1,0:T(4,128)} %param.10) | copy-start | bytes 24580
  174.9 80.2 %copy-start.4 = (f32[4,512]{1,0:T(4,128)S(1)}, f32[4,512]{1,0:T(4,128)}, u32[]{:S(2)}) copy-start(f32[4,512]{1,0:T(4,128)} %param.8) | copy-start | bytes 24580
  176.9 332.0 %reduce-scatter.19.cloned.1.call-start = ((), (), s32[]{:S(2)}) async-start(), calls=%async_computation.7 | async-start | bytes 2228224
  423.9 3.5 copy-start.2
  430.0 167.2 %reduce-scatter.15.cloned.1.call-start = ((), (), s32[]{:S(2)}) async-start(), calls=%async_computation.5 | async-start | bytes 2228224
Sparse Core Ops, SparseCore 0:
  88.2 78.6 reduce-scatter.16
  177.0 78.1 reduce-scatter.12
  430.1 78.6 reduce-scatter.18
  518.9 78.2 reduce-scatter.14
where the time goes:
time: 658 us; the launch traced here: 657 us
  waiting for transfers between devices  313 us (48%)
  blocking collectives  275 us (42%)
  matrix products  31.7 us (5%)
  between operations  23.1 us (4%)
  local copies, waits for them, and re-layouts  10.9 us (2%)
    unnamed x8, waiting for transfers between devices  313 us
    psum x2, blocking collectives, genomic_map(): mapped = lax.psum(partial_map, 'cores')  136 us
    psum x2, blocking collectives, residual_inner(): return lax.psum(local_sum, ('grp', 'cores'))  86.5 us
    psum x1, blocking collectives, body(): step_size = rz_now / lax.psum(local_curve, ('grp', 'cores'))  48.1 us
  transfers between devices with their start and end apart: 4, of which 4 were waited for; matrix products, arithmetic and copies ran while one was open for 0% of the time, Pallas kernels for 0%

commit v1 on v0

--- a/solution.py
+++ b/solution.py
@@ -9,7 +9,9 @@
 def genomic_map(core_vec, non_vec, core_inverse, genomic_block, m_inverse):
     core_in = core_vec.astype(jnp.bfloat16)
     partial_map = jnp.dot(core_in, core_inverse, preferred_element_type=jnp.float32)
-    mapped = lax.psum(partial_map, "cores")
+    mapped = partial_map
+    for hop in (1, 2, 4, 8):
+        mapped = mapped + lax.ppermute(mapped, "cores", [(dev, dev ^ hop) for dev in range(16)])
     mapped_in = mapped.astype(jnp.bfloat16)
     pulled = lax.dot_general(
         mapped_in, genomic_block, (((1,), (1,)), ((), ())), preferred_element_type=jnp.float32

time: 658 us -> 554 us (0.84)
  blocking collectives: 275 us -> 140 us
  waiting for transfers between devices: 313 us -> 337 us
  starting transfers between devices: 0.16 us -> 11.2 us
    psum x2 -> x0, blocking collectives: 136 us -> none  [genomic_map(): mapped = lax.psum(partial_map, 'cores')]
    ppermute x0 -> x8, waiting for transfers between devices: none -> 32.9 us  [genomic_map(): lax.ppermute(mapped, 'cores', [(dev, dev ^ hop) for dev in range(16)])]
    ppermute x0 -> x8, starting transfers between devices: none -> 11 us  [genomic_map(): lax.ppermute(mapped, 'cores', [(dev, dev ^ hop) for dev in range(16)])]
    unnamed x8, waiting for transfers between devices: 313 us -> 304 us
  transfers between devices with their start and end apart: 4 -> 12, of which waited for: 4 -> 12; matrix products, arithmetic and copies ran while one was open for 0% -> 0% of each run, Pallas kernels for 0% -> 0%
where the time goes in v1:
time: 554 us; the launch traced here: 553 us
  waiting for transfers between devices  337 us (61%)
  blocking collectives  140 us (25%)
  matrix products  27.2 us (5%)
  between operations  23.1 us (4%)
  starting transfers between devices  11.2 us (2%)
  local copies, waits for them, and re-layouts  10.9 us (2%)
    unnamed x8, waiting for transfers between devices  304 us
    psum x2, blocking collectives, residual_inner(): return lax.psum(local_sum, ('grp', 'cores'))  86.7 us
    psum x1, blocking collectives, body(): step_size = rz_now / lax.psum(local_curve, ('grp', 'cores'))  48.4 us
    ppermute x8, waiting for transfers between devices, genomic_map(): lax.ppermute(mapped, 'cores', [(dev, dev ^ hop) for dev in range(16)])  32.9 us
  transfers between devices with their start and end apart: 12, of which 12 were waited for; matrix products, arithmetic and copies ran while one was open for 0% of the time, Pallas kernels for 0%

profile of v1, /device:TPU:12, one launch (start us, length us, event | category | flops | bytes accessed | tf_op | source)
XLA Modules:
  0.0 552.8 jit_solution(3654001375441041993)
XLA Ops:
  9.3 4.7 fusion.10
  15.6 3.7 collective-permute-done
  19.9 4.5 collective-permute-done.1
  24.9 4.5 collective-permute-done.2
  29.5 2.7 collective-permute-start.3
  32.2 3.8 collective-permute-done.3
  39.9 74.4 %reduce-scatter.17.cloned.1.call-done = bf16[512,4]{1,0:T(8,128)(2,1)} async-done(((bf16[8192,4]{1,0:T(8,128)(2,1)}), bf16[512,4]{1,0:T(8,128)(2,1)}) %reduce-scatter.17.cloned.1.call-update) | async-done | bytes 4112
  115.2 2.5 psum.48
  117.7 4.6 convolution_convert_fusion.2
  122.3 1.9 copy.12
  125.0 77.5 %reduce-scatter.13.cloned.1.call-done = bf16[512,4]{1,0:T(8,128)(2,1)} async-done(((bf16[8192,4]{1,0:T(8,128)(2,1)}), bf16[512,4]{1,0:T(8,128)(2,1)}) %reduce-scatter.13.cloned.1.call-update) | async-done | bytes 4112
  206.8 48.5 %all-reduce = (f32[]{:T(128)}, f32[]{:T(128)}) all-reduce(f32[]{:T(128)S(6)} %add.98, f32[]{:T(128)S(6)} %add.105), channel_id=1, replica_groups=mesh['grp'=2,'cores'=16] {'grp','cores'}, use_global_device_ids=true, to_apply=%region_2.3 | all-reduce | flops 2 | bytes 16 | tf_op jit(solution)/shard_map/psum | solution.py:56
  259.3 38.3 %psum.45 = f32[]{:T(128)} all-reduce(f32[]{:T(128)S(6)} %add.106), channel_id=1, replica_groups=mesh['grp'=2,'cores'=16] {'grp','cores'}, use_global_device_ids=true, to_apply=%region_11.12 | all-reduce | flops 1 | bytes 8 | tf_op jit(solution)/shard_map/psum | solution.py:56
  298.9 4.7 fusion.8
  305.5 3.1 collective-permute-done.4
  308.9 4.9 collective-permute-done.5
  313.8 2.2 collective-permute-start.6
  315.9 3.9 collective-permute-done.6
  321.5 4.4 collective-permute-done.7
  329.7 74.6 %reduce-scatter.19.cloned.1.call-done = bf16[512,4]{1,0:T(8,128)(2,1)} async-done(((bf16[8192,4]{1,0:T(8,128)(2,1)}), bf16[512,4]{1,0:T(8,128)(2,1)}) %reduce-scatter.19.cloned.1.call-update) | async-done | bytes 4112
  405.3 2.5 psum.49
  407.8 4.6 convolution_convert_fusion
  415.0 77.2 %reduce-scatter.15.cloned.1.call-done = bf16[512,4]{1,0:T(8,128)(2,1)} async-done(((bf16[8192,4]{1,0:T(8,128)(2,1)}), bf16[512,4]{1,0:T(8,128)(2,1)}) %reduce-scatter.15.cloned.1.call-update) | async-done | bytes 4112
  495.3 48.4 %psum.47 = f32[]{:T(128)} all-reduce(f32[]{:T(128)S(6)} %add.115), channel_id=1, replica_groups=mesh['grp'=2,'cores'=16] {'grp','cores'}, use_global_device_ids=true, to_apply=%region_17.18 | all-reduce | flops 1 | bytes 8 | tf_op jit(solution)/shard_map/psum | solution.py:64
  (59 shorter events, 27.8 us)
Async XLA Ops:
  7.2 0.7 copy-start
  7.2 107.1 %reduce-scatter.17.cloned.1.call-start = ((), (), s32[]{:S(2)}) async-start(), calls=%async_computation.6 | async-start | bytes 2228224
  9.3 22.9 %copy-start.5 = (f32[4,256]{1,0:T(4,128)S(1)}, f32[4,256]{1,0:T(4,128)}, u32[]{:S(2)}) copy-start(f32[4,256]{1,0:T(4,128)} %param.11) | copy-start | bytes 12292
  9.3 22.9 %copy-start.6 = (f32[4,256]{1,0:T(4,128)S(1)}, f32[4,256]{1,0:T(4,128)}, u32[]{:S(2)}) copy-start(f32[4,256]{1,0:T(4,128)} %param.9) | copy-start | bytes 12292
  9.3 22.8 %copy-start.7 = (f32[256]{0:T(256)S(1)}, f32[256]{0:T(256)}, u32[]{:S(2)}) copy-start(f32[256]{0:T(256)} %param.14) | copy-start | bytes 3076
  9.3 26.7 %copy-start.1 = (bf16[256,8192]{1,0:T(8,128)(2,1)S(1)}, bf16[256,8192]{1,0:T(8,128)(2,1)}, u32[]{:S(2)}) copy-start(bf16[256,8192]{1,0:T(8,128)(2,1)} %param.13) | copy-start | bytes 12582916
  14.1 5.2 collective-permute-start
  19.3 5.0 collective-permute-start.1
  24.4 5.0 collective-permute-start.2
  29.5 6.5 %collective-permute-start.3 = (f32[4,8192]{1,0:T(4,128)S(1)}, f32[4,8192]{1,0:T(4,128)S(1)}, u32[]{:S(2)}, u32[]{:S(2)}) collective-permute-start(f32[4,8192]{1,0:T(4,128)S(1)} %add.101), channel_id=1, source_target_pairs={{0,8},{1,9},{2,10},{3,11},{4,12},{5,13},{6,14},{7,15},{8,0},{9,1},... | collective-permute-start | bytes 393224 | tf_op jit(solution)/shard_map/ppermute | solution.py:14
  39.8 162.7 %reduce-scatter.13.cloned.1.call-start = ((), (), s32[]{:S(2)}) async-start(), calls=%async_computation.4 | async-start | bytes 2228224
  122.3 80.2 %copy-start.3 = (f32[4,512]{1,0:T(4,128)S(1)}, f32[4,512]{1,0:T(4,128)}, u32[]{:S(2)}) copy-start(f32[4,512]{1,0:T(4,128)} %param.10) | copy-start | bytes 24580
  122.3 80.2 %copy-start.4 = (f32[4,512]{1,0:T(4,128)S(1)}, f32[4,512]{1,0:T(4,128)}, u32[]{:S(2)}) copy-start(f32[4,512]{1,0:T(4,128)} %param.8) | copy-start | bytes 24580
  124.2 280.2 %reduce-scatter.19.cloned.1.call-start = ((), (), s32[]{:S(2)}) async-start(), calls=%async_computation.7 | async-start | bytes 2228224
  298.9 27.0 %copy-start.2 = (bf16[256,8192]{1,0:T(8,128)(2,1)S(1)}, bf16[256,8192]{1,0:T(8,128)(2,1)}, u32[]{:S(2)}) copy-start(bf16[256,8192]{1,0:T(8,128)(2,1)} %param.13) | copy-start | bytes 12582916
  303.7 5.0 collective-permute-start.4
  308.7 5.0 collective-permute-start.5
  313.8 6.1 %collective-permute-start.6 = (f32[4,8192]{1,0:T(4,128)S(1)}, f32[4,8192]{1,0:T(4,128)S(1)}, u32[]{:S(2)}, u32[]{:S(2)}) collective-permute-start(f32[4,8192]{1,0:T(4,128)S(1)} %add.110), channel_id=1, source_target_pairs={{0,4},{1,5},{2,6},{3,7},{4,0},{5,1},{6,2},{7,3},{8,12},{9,13},{10,... | collective-permute-start | bytes 393224 | tf_op jit(solution)/shard_map/ppermute | solution.py:14
  319.9 6.0 %collective-permute-start.7 = (f32[4,8192]{1,0:T(4,128)S(1)}, f32[4,8192]{1,0:T(4,128)S(1)}, u32[]{:S(2)}, u32[]{:S(2)}) collective-permute-start(f32[4,8192]{1,0:T(4,128)S(1)} %add.111), channel_id=1, source_target_pairs={{0,8},{1,9},{2,10},{3,11},{4,12},{5,13},{6,14},{7,15},{8,0},{9,1},... | collective-permute-start | bytes 393224 | tf_op jit(solution)/shard_map/ppermute | solution.py:14
  329.7 162.5 %reduce-scatter.15.cloned.1.call-start = ((), (), s32[]{:S(2)}) async-start(), calls=%async_computation.5 | async-start | bytes 2228224
Sparse Core Ops, SparseCore 0:
  39.9 74.2 reduce-scatter.16
  124.3 78.1 reduce-scatter.12
  329.8 74.4 reduce-scatter.18
  414.4 77.7 reduce-scatter.14
